TPU v7x, 32 devices: a whole 2x2x4 slice. The times are simulated.
32 devices in a mesh: grp: 8 (over z, x), nbr: 4 (over y, core).
Axes of the slice: x: 2, y: 2, z: 4, core: 2. Of those that a mesh axis runs over, the one named last changes fastest.
Arguments:
- gains: float32 [128, 256, 256], P(('grp', 'nbr')), may hold values from -1 to 1
- covs: float32 [128, 256, 256], P(('grp', 'nbr')), may hold values from -10 to 10, as said below
- terminal: float32 [256, 256], replicated, may hold values from -4 to 4, as said below
Outputs:
- smoothed: float32 [128, 256, 256], P(('grp', 'nbr'))
Inputs may be any that keep to these rules, and one draw needn't show every extreme that they name: `covs`: each matrix is symmetric positive definite. `terminal`: symmetric positive definite.
All inputs are finite; a program needn't handle non-finite values.
Results may differ from a plain program's by a relative error of at most 0.0003.
Values sent between devices are 32-bit elements; how exact they have to be, the bound alone decides.
A program may use at most 64 MiB of HBM per device.

v0:
```python
import jax
import jax.numpy as jnp
from jax import lax
from jax.sharding import PartitionSpec as P


def entering(x, axis, combine, identity):
    length, place = (lax.axis_size(axis), lax.axis_index(axis))
    everything = jax.tree.map(lambda part: lax.all_gather(part, axis), x)
    start = jax.tree.map(
        lambda part, zero: jnp.broadcast_to(jnp.asarray(zero, part.dtype), part.shape), x, identity
    )

    def step(k, before):
        at = length - 1 - k
        reached = at > place
        new = combine(before, jax.tree.map(lambda part: part[at], everything))
        return jax.tree.map(lambda a, b: jnp.where(reached, a, b), new, before)

    return lax.fori_loop(0, length, step, start)


def matmul(left, right):
    return jnp.matmul(
        left, right, precision=lax.Precision.HIGHEST, preferred_element_type=jnp.float32
    )


def matmul_tr(left, right):
    return jnp.matmul(
        left,
        jnp.swapaxes(right, -1, -2),
        precision=lax.Precision.HIGHEST,
        preferred_element_type=jnp.float32,
    )


def compose(first, second):
    gain_a, cov_a = first
    gain_b, cov_b = second
    mixed = matmul(gain_a, cov_b)
    return (matmul(gain_a, gain_b), matmul_tr(mixed, gain_a) + cov_a)


def combine(earlier, later):
    return compose(later, earlier)


def suffixes(stack_gain, stack_cov, identity):
    inc_gain, inc_cov = lax.associative_scan(combine, (stack_gain, stack_cov), reverse=True)
    padded_gain = jnp.concatenate([inc_gain, identity[0][None]], axis=0)
    padded_cov = jnp.concatenate([inc_cov, identity[1][None]], axis=0)
    return (padded_gain, padded_cov)


def per_device(gains, covs, terminal):
    count = gains.shape[0]
    width = gains.shape[1]
    identity = (jnp.eye(width, dtype=jnp.float32), jnp.zeros((width, width), jnp.float32))
    total = (gains[count - 1], covs[count - 1])
    for step in range(count - 2, -1, -1):
        total = compose((gains[step], covs[step]), total)
    every_gain, every_cov = (
        lax.all_gather(total[0][None], "nbr", axis=0, tiled=True),
        lax.all_gather(total[1][None], "nbr", axis=0, tiled=True),
    )
    position = lax.axis_index("nbr")
    padded_gain, padded_cov = suffixes(every_gain, every_cov, identity)
    after = (
        lax.dynamic_index_in_dim(padded_gain, position + 1, 0, keepdims=False),
        lax.dynamic_index_in_dim(padded_cov, position + 1, 0, keepdims=False),
    )
    group_total = (padded_gain[0], padded_cov[0])
    beyond = entering(group_total, "grp", combine, identity)
    suffix = compose(after, beyond)
    state = matmul_tr(matmul(suffix[0], terminal), suffix[0]) + suffix[1]
    results = []
    for step in range(count - 1, -1, -1):
        state = matmul_tr(matmul(gains[step], state), gains[step]) + covs[step]
        results.append(state)
    return jnp.stack(results[::-1], axis=0)


def solution(mesh):
    placed = (P(("grp", "nbr"), None, None), P(("grp", "nbr"), None, None), P())
    return jax.shard_map(
        per_device,
        mesh=mesh,
        in_specs=placed,
        out_specs=P(("grp", "nbr"), None, None),
        check_vma=False,
    )
```

profile of v0, /device:TPU:0, one launch (start us, length us, event | category | flops | bytes accessed | tf_op | source)
XLA Modules:
  0.0 214.9 jit_solution(14780132625737845264)
XLA Ops:
  6.5 1.6 fusion.38
  8.1 1.4 convolution_add_fusion.10
  9.6 1.5 fusion.53
  12.4 1.3 convolution_add_fusion.8
  14.7 1.1 convolution_bitcast_fusion.3
  15.9 17.3 %all-gather.13.cloned.1.call-done = f32[1024,256]{1,0:T(8,128)} async-done(((f32[256,256]{1,0:T(8,128)}), f32[1024,256]{1,0:T(8,128)}) %all-gather.13.cloned.1.call-update) | async-done | bytes 1048592 | tf_op jit(solution)/shard_map/all_gather | solution.py:65
  33.3 1.9 slice.131
  35.1 16.4 %all-gather.11.cloned.1.call-done = f32[1024,256]{0,1:T(8,128)} async-done(((f32[256,256]{0,1:T(8,128)}), f32[1024,256]{0,1:T(8,128)}) %all-gather.11.cloned.1.call-update) | async-done | bytes 1048592 | tf_op jit(solution)/shard_map/all_gather | solution.py:64
  51.6 1.6 copy.18
  53.9 2.5 %fusion.19 = f32[2,256,256]{2,1,0:T(8,128)} fusion(f32[2,256,256]{2,1,0:T(8,128)S(1)} %slice.117, f32[4,256,256]{2,1,0:T(8,128)} %bitcast.169), kind=kOutput, calls=%fused_computation.47 | convolution fusion | flops 402653184 | bytes 1572864 | tf_op jit(solution)/shard_map/dot_general | solution.py:24
  57.4 1.7 convolution_add_fusion.1
  62.6 2.8 %pad.33 = f32[4,256,256]{2,1,0:T(8,128)} pad(f32[2,256,256]{2,1,0:T(8,128)} %pad_maximum_fusion.2, f32[]{:T(128)} %constant.60.clone.1), padding=0_1_1x0_0_0x0_0_0 | pad | bytes 1572868 | tf_op jit(solution)/shard_map/pad | solution.py:50
  65.5 1.7 slice_add_fusion
  68.2 1.3 convolution_bitcast_fusion.1
  70.6 1.8 pad.29
  72.4 1.8 pad.30
  74.2 1.1 slice_add_fusion.1
  76.2 2.5 %add.129 = f32[4,256,256]{2,1,0:T(8,128)} add(f32[4,256,256]{2,1,0:T(8,128)} %pad.33, f32[4,256,256]{2,1,0:T(8,128)S(1)} %copy-done.3) | non-fusion elementwise | flops 262144 | bytes 3145728 | tf_op jit(solution)/shard_map/add | solution.py:50
  78.7 1.1 add.119
  80.3 1.1 rev.9
  81.4 1.3 rev.8
  82.8 33.6 %all-gather.9.cloned.1.call-done = f32[8,256,256]{2,1,0:T(8,128)} async-done(((f32[1,256,256]{2,1,0:T(8,128)}), f32[8,256,256]{2,1,0:T(8,128)}) %all-gather.9.cloned.1.call-update) | async-done | bytes 2097168 | tf_op jit(solution)/shard_map/all_gather | solution.py:9
  116.4 49.6 %all-gather.7.cloned.1.call-done = f32[8,256,256]{2,1,0:T(8,128)} async-done(((f32[1,256,256]{2,1,0:T(8,128)}), f32[8,256,256]{2,1,0:T(8,128)}) %all-gather.7.cloned.1.call-update) | async-done | bytes 2097168 | tf_op jit(solution)/shard_map/all_gather | solution.py:9
  166.1 33.9 %while.18 = (s32[]{:T(128)}, f32[256,256]{1,0:T(8,128)S(1)}, f32[256,256]{1,0:T(8,128)S(1)}, s32[]{:T(128)}, f32[8,256,256]{2,1,0:T(8,128)}, /*index=5*/f32[8,25...) while((s32[]{:T(128)}, f32[256,256]{1,0:T(8,128)S(1)}, f32[256,256]{1,0:T(8,128)S(1)}, ...), condition=%wide.region_1.2_spmd.clone, body=%wide.region_0.1_spmd.clone.sunk | while | flops 604307456 | bytes 3672247 | solution.py:20
  166.1 1.3 convolution_select_fusion.2
  167.4 1.3 fusion.150
  168.8 1.5 fusion.151
  170.3 1.3 convolution_select_fusion.2
  171.7 1.3 fusion.150
  173.0 1.5 fusion.151
  174.6 1.3 convolution_select_fusion.2
  175.9 1.3 fusion.150
  177.3 1.5 fusion.151
  178.8 1.3 convolution_select_fusion.2
  180.2 1.3 fusion.150
  181.5 1.5 fusion.151
  183.1 1.3 convolution_select_fusion.2
  184.4 1.3 fusion.150
  185.8 1.5 fusion.151
  187.3 1.3 convolution_select_fusion.2
  188.7 1.3 fusion.150
  190.0 1.5 fusion.151
  191.6 1.3 convolution_select_fusion.2
  192.9 1.3 fusion.150
  194.2 1.5 fusion.151
  195.8 1.3 convolution_select_fusion.2
  197.1 1.3 fusion.150
  198.5 1.5 fusion.151
  (82 shorter events, 19.3 us)
Async XLA Ops:
  6.5 194.7 %copy-start = (f32[256,256]{1,0:T(8,128)S(1)}, f32[256,256]{1,0:T(8,128)}, u32[]{:S(2)}) copy-start(f32[256,256]{1,0:T(8,128)} %param.7) | copy-start | bytes 786436
  6.5 4.6 %copy-start.1 = (f32[4,256,256]{2,1,0:T(8,128)S(1)}, f32[4,256,256]{2,1,0:T(8,128)}, u32[]{:S(2)}) copy-start(f32[4,256,256]{2,1,0:T(8,128)} %param.5) | copy-start | bytes 3145732
  6.5 4.6 %copy-start.9 = (f32[4,256,256]{2,1,0:T(8,128)S(1)}, f32[4,256,256]{2,1,0:T(8,128)}, u32[]{:S(2)}) copy-start(f32[4,256,256]{2,1,0:T(8,128)} %param.6) | copy-start | bytes 3145732
  6.5 26.7 %all-gather.13.cloned.1.call-start = ((), (), s32[]{:S(2)}) async-start(), calls=%async_computation.3 | async-start | bytes 1310720 | tf_op jit(solution)/shard_map/all_gather | solution.py:65
  13.7 37.9 %all-gather.11.cloned.1.call-start = ((), (), s32[]{:S(2)}) async-start(), calls=%async_computation.2 | async-start | bytes 1310720 | tf_op jit(solution)/shard_map/all_gather | solution.py:64
  15.9 100.6 %all-gather.9.cloned.1.call-start = ((), (), s32[]{:S(2)}) async-start(), calls=%async_computation.1 | async-start | bytes 2359296 | tf_op jit(solution)/shard_map/all_gather | solution.py:9
  59.2 1.2 copy-start.11
  59.2 1.5 copy-start.8
  62.6 5.6 %copy-start.2 = (f32[4,256,256]{2,1,0:T(8,128)}, f32[4,256,256]{2,1,0:T(8,128)S(1)}, u32[]{:S(2)}) copy-start(f32[4,256,256]{2,1,0:T(8,128)S(1)} %pad.34) | copy-start | bytes 3145732
  67.2 98.9 %all-gather.7.cloned.1.call-start = ((), (), s32[]{:S(2)}) async-start(), calls=%async_computation | async-start | bytes 2359296 | tf_op jit(solution)/shard_map/all_gather | solution.py:9
  72.4 3.8 %copy-start.3 = (f32[4,256,256]{2,1,0:T(8,128)S(1)}, f32[4,256,256]{2,1,0:T(8,128)}, u32[]{:S(2)}) copy-start(f32[4,256,256]{2,1,0:T(8,128)} %copy-done.2) | copy-start | bytes 3145732
  76.1 2.6 %copy-start.4 = (f32[4,256,256]{1,2,0:T(8,128)S(1)}, f32[4,256,256]{1,2,0:T(8,128)}, u32[]{:S(2)}) copy-start(f32[4,256,256]{1,2,0:T(8,128)} %pad.29) | copy-start | bytes 3145732
  76.2 2.6 %copy-start.5 = (f32[4,256,256]{1,2,0:T(8,128)S(1)}, f32[4,256,256]{1,2,0:T(8,128)}, u32[]{:S(2)}) copy-start(f32[4,256,256]{1,2,0:T(8,128)} %pad.30) | copy-start | bytes 3145732
  78.7 1.6 copy-start.6
  200.0 2.0 copy-start.7
  201.2 1.8 copy-start.10
Sparse Core Ops, SparseCore 0:
  13.8 19.4 all-gather.12
  34.8 16.6 all-gather.10
  67.3 49.0 all-gather.8
  118.4 47.6 all-gather.6
where the time goes:
time: 216 us; the launch traced here: 215 us
  waiting for transfers between devices  117 us (54%)
  matrix products  58.2 us (27%)
  local copies, waits for them, and re-layouts  16.8 us (8%)
  between operations  13.6 us (6%)
  other arithmetic  8.45 us (4%)
    all_gather x2, waiting for transfers between devices, entering(): everything = jax.tree.map(lambda part: lax.all_gather(part, axis), x)  83.3 us
    dot_general x35, matrix products, matmul(): jnp.matmul(left, right, precision=lax.Precision.HIGHEST, preferred_elemen...  37.2 us
    dot_general x20, matrix products, matmul_tr(): jnp.matmul(left, jnp.swapaxes(right, -1, -2), precision=lax.Precision.HIG...  21 us
    all_gather x1, waiting for transfers between devices, per_device(): lax.all_gather(total[1][None], 'nbr', axis=0, tiled=True)  17.3 us
    all_gather x1, waiting for transfers between devices, per_device(): lax.all_gather(total[0][None], 'nbr', axis=0, tiled=True)  16.4 us
    pad x4, local copies, waits for them, and re-layouts, suffixes(): lax.associative_scan(combine, (stack_gain, stack_cov), reverse=True)  6.52 us
    add x6, other arithmetic, suffixes(): lax.associative_scan(combine, (stack_gain, stack_cov), reverse=True)  6.44 us
  transfers between devices with their start and end apart: 4, of which 4 were waited for; matrix products, arithmetic and copies ran while one was open for 9% of the time, Pallas kernels for 0%

commit v1 on v0

v1 whole, which is shorter than its diff:
```python
import functools

import jax
import jax.numpy as jnp
from jax import lax
from jax.experimental import pallas as pl
from jax.experimental.pallas import tpu as pltpu
from jax.sharding import PartitionSpec as P

MESH = pl.DeviceIdType.MESH
F32, BF16 = jnp.float32, jnp.bfloat16
NN = (((1,), (0,)), ((), ()))
NT = (((1,), (1,)), ((), ()))


def halves(a):
    high = a.astype(BF16)
    return high, (a - high.astype(F32)).astype(BF16)


def left_form(a):
    high, low = halves(a)
    return jnp.concatenate([high, high, low], axis=1)


def right_form(b):
    high, low = halves(b)
    return jnp.concatenate([high, low, high], axis=0)


def right_form_tr(b):
    high, low = halves(b)
    return jnp.concatenate([high, low, high], axis=1)


def product(a, b):
    return lax.dot_general(a, b, NN, preferred_element_type=F32)


def product_tr(a, b):
    return lax.dot_general(a, b, NT, preferred_element_type=F32)


def congruence(gain, cov, state):
    mixed = product(left_form(gain), right_form(state))
    return product_tr(left_form(mixed), right_form_tr(gain)) + cov


def compose(first, second):
    gain = product(left_form(first[0]), right_form(second[0]))
    return gain, congruence(first[0], first[1], second[1])


def tree(pairs):
    while len(pairs) > 1:
        nxt = [compose(pairs[i], pairs[i + 1]) for i in range(0, len(pairs) - 1, 2)]
        if len(pairs) % 2:
            nxt.append(pairs[-1])
        pairs = nxt
    return pairs[0]


def kernel(groups, nbrs, g_ref, c_ref, t_ref, o_ref, tot, suf, loc, fin, state, out_state, beyond, ssem, rsem):
    count, width = g_ref.shape[0], g_ref.shape[1]
    half = width // 2
    quarter_len = groups // 4
    g, n = lax.axis_index("grp"), lax.axis_index("nbr")
    core = lax.rem(n, 2)
    quarter = g // quarter_len
    mate = (g, n + 1 - 2 * core)
    mine = pl.ds(pl.multiple_of(core * half, half), half)

    levels = []
    step = 1
    while step < nbrs:
        bit = lax.rem(n // step, 2)
        levels.append((bit, (g, n + step * (1 - 2 * bit))))
        step *= 2
    step = 1
    while step < quarter_len:
        bit = lax.rem(g // step, 2)
        levels.append((bit, (g + step * (1 - 2 * bit), n)))
        step *= 2
    down = (lax.rem(g + 3 * quarter_len, groups), n)
    up = (lax.rem(g + quarter_len, groups), n)

    barrier = pltpu.get_barrier_semaphore()
    greeted = [partner for _, partner in levels] + [down, up]
    for other in greeted:
        pl.semaphore_signal(barrier, inc=1, device_id=other, device_id_type=MESH)

    sems = iter(range(ssem.shape[0]))

    def copy(src, dst, to, sem):
        return pltpu.make_async_remote_copy(
            src_ref=src, dst_ref=dst, send_sem=ssem.at[sem], recv_sem=rsem.at[sem],
            device_id=to, device_id_type=MESH,
        )

    first_bit = levels[0][0]
    pairs = [(g_ref[k], c_ref[k]) for k in range(count)]
    gain, cov = tree(pairs)
    tot[0, first_bit, 0] = gain
    tot[0, first_bit, 1] = cov
    pl.semaphore_wait(barrier, len(greeted))

    pending = []
    for at, (bit, partner) in enumerate(levels):
        moved, passed = [], []
        for part in range(2):
            sem = next(sems)
            if at == 0:
                ref = tot.at[at, bit, part]
                moved.append(copy(ref, ref, partner, sem))
            else:
                ref = tot.at[at, bit, part, mine]
                moved.append(copy(ref, ref, partner, sem))
                sem = next(sems)
                ref = tot.at[at, 1 - bit, part, mine]
                passed.append(copy(ref, ref, mate, sem))
        for one in moved:
            one.start()
        if at == 0:
            own = (g_ref[count - 1], c_ref[count - 1])
            for k in range(count - 1, 0, -1):
                if k < count - 1:
                    own = compose((g_ref[k], c_ref[k]), own)
                loc[k, 0], loc[k, 1] = own
            loc[0, 0], loc[0, 1] = tot[0, first_bit, 0], tot[0, first_bit, 1]
            rows = lax.broadcasted_iota(jnp.int32, (width, width), 0)
            columns = lax.broadcasted_iota(jnp.int32, (width, width), 1)
            suf[0] = jnp.where(rows == columns, F32(1), F32(0))
            suf[1] = jnp.zeros((width, width), F32)
        else:
            @pl.when(levels[at - 1][0] == 0)
            def _():
                new = compose((suf[0], suf[1]), (tot[at - 1, 1, 0], tot[at - 1, 1, 1]))
                suf[0], suf[1] = new
        for i, one in enumerate(moved):
            one.wait_recv()
            if passed:
                passed[i].start()
        if passed:
            for one in passed:
                one.wait_recv()
        pending += moved + passed
        new = compose((tot[at, 0, 0], tot[at, 0, 1]), (tot[at, 1, 0], tot[at, 1, 1]))
        slot = levels[at + 1][0] if at + 1 < len(levels) else 0
        tot[at + 1, slot, 0], tot[at + 1, slot, 1] = new

    last = len(levels)
    total = tot.at[last, 0]

    pair_sems = [next(sems) for _ in range(4)]
    state_sem, state_pass_sem = next(sems), next(sems)
    send_pair = [copy(total.at[i, mine], beyond.at[i, mine], down, pair_sems[i]) for i in range(2)]
    pass_pair = [copy(beyond.at[i, mine], beyond.at[i, mine], mate, pair_sems[2 + i]) for i in range(2)]
    send_state = copy(out_state.at[mine], state.at[mine], down, state_sem)
    relay_state = copy(state.at[mine], state.at[mine], down, state_sem)
    pass_state = copy(state.at[mine], state.at[mine], mate, state_pass_sem)

    def finish_suffix():
        @pl.when(levels[-1][0] == 0)
        def _():
            new = compose((suf[0], suf[1]), (tot[last - 1, 1, 0], tot[last - 1, 1, 1]))
            suf[0], suf[1] = new

    def finals():
        for k in range(count):
            new = compose((loc[k, 0], loc[k, 1]), (suf[0], suf[1]))
            fin[k, 0], fin[k, 1] = new

    @pl.when(quarter == 3)
    def _():
        out_state[...] = congruence(total[0], total[1], t_ref[...])
        send_state.start()
        state[...] = t_ref[...]
        finish_suffix()
        finals()
        send_state.wait_send()

    @pl.when(quarter == 2)
    def _():
        finish_suffix()
        send_state.wait_recv()
        pass_state.start()
        pass_state.wait_recv()
        out_state[...] = congruence(total[0], total[1], state[...])
        send_state.start()
        finals()
        pass_state.wait_send()
        send_state.wait_send()

    @pl.when(quarter == 1)
    def _():
        for one in send_pair:
            one.start()
        finish_suffix()
        finals()
        relay_state.wait_recv()
        relay_state.start()
        pass_state.start()
        pass_state.wait()
        for one in send_pair:
            one.wait_send()
        relay_state.wait_send()

    @pl.when(quarter == 0)
    def _():
        finish_suffix()
        for i, one in enumerate(send_pair):
            one.wait_recv()
            pass_pair[i].start()
        for one in pass_pair:
            one.wait()
        suf[0], suf[1] = compose((suf[0], suf[1]), (beyond[0], beyond[1]))
        finals()
        relay_state.wait_recv()
        pass_state.start()
        pass_state.wait()

    entering = right_form(state[...])
    for k in range(count):
        mixed = product(left_form(fin[k, 0]), entering)
        o_ref[k] = product_tr(left_form(mixed), right_form_tr(fin[k, 0])) + fin[k, 1]

    for one in pending:
        one.wait_send()


def solution(mesh):
    groups, nbrs = mesh.shape["grp"], mesh.shape["nbr"]
    levels = (nbrs.bit_length() - 1) + ((groups // 4).bit_length() - 1)
    n_sems = 2 + 4 * (levels - 1) + 6

    def per_device(gains, covs, terminal):
        count, width = gains.shape[0], gains.shape[1]
        pair = (2, width, width)
        vmem = pl.BlockSpec(memory_space=pltpu.VMEM)
        return pl.pallas_call(
            functools.partial(kernel, groups, nbrs),
            out_shape=jax.ShapeDtypeStruct(gains.shape, F32),
            in_specs=[vmem] * 3,
            out_specs=vmem,
            scratch_shapes=[
                pltpu.VMEM((levels + 1, 2) + pair, F32),
                pltpu.VMEM(pair, F32),
                pltpu.VMEM((count,) + pair, F32),
                pltpu.VMEM((count,) + pair, F32),
                pltpu.VMEM((width, width), F32),
                pltpu.VMEM((width, width), F32),
                pltpu.VMEM(pair, F32),
                pltpu.SemaphoreType.DMA((n_sems,)),
                pltpu.SemaphoreType.DMA((n_sems,)),
            ],
            compiler_params=pltpu.CompilerParams(collective_id=0, has_side_effects=True),
        )(gains, covs, terminal)

    placed = P(("grp", "nbr"), None, None)
    return jax.shard_map(
        per_device, mesh=mesh, in_specs=(placed, placed, P()), out_specs=placed, check_vma=False
    )
```

time: 216 us -> 51.6 us (0.24)
  waiting for transfers between devices: 117 us -> 0 us
  matrix products: 58.2 us -> 0 us
  Pallas kernels: 0 us -> 49.1 us
  local copies, waits for them, and re-layouts: 16.8 us -> 2.29 us
  between operations: 13.6 us -> 0.01 us
  other arithmetic: 8.45 us -> 0 us
    all_gather x4 -> x0, waiting for transfers between devices: 117 us -> none  [the longest x2 83.3 us: entering(): everything = jax.tree.map(lambda part: lax.all_gather(part, axis), x)]
    dot_general x55 -> x0, matrix products: 58.2 us -> none  [the longest x35 37.2 us: matmul(): jnp.matmul(left, right, precision=lax.Precision.HIGHEST, preferred_elemen...]
    pallas_call x0 -> x1, Pallas kernels: none -> 49.1 us  [per_device(): pl.pallas_call(functools.partial(kernel, groups, nbrs), out_shape=jax.Sha...]
    pad x4 -> x0, local copies, waits for them, and re-layouts: 6.52 us -> none  [suffixes(): lax.associative_scan(combine, (stack_gain, stack_cov), reverse=True)]
    add x6 -> x0, other arithmetic: 6.44 us -> none  [suffixes(): lax.associative_scan(combine, (stack_gain, stack_cov), reverse=True)]
    slice x9 -> x0, local copies, waits for them, and re-layouts: 4.87 us -> none  [the longest x8 4.04 us: suffixes(): lax.associative_scan(combine, (stack_gain, stack_cov), reverse=True)]
    rev x2 -> x0, local copies, waits for them, and re-layouts: 2.38 us -> none  [suffixes(): lax.associative_scan(combine, (stack_gain, stack_cov), reverse=True)]
  transfers between devices with their start and end apart: 4 -> 0, of which waited for: 4 -> 0; matrix products, arithmetic and copies ran while one was open for 9% -> 0% of each run, Pallas kernels for 0% -> 0%
where the time goes in v1:
time: 51.6 us; the launch traced here: 51.4 us
  Pallas kernels  49.1 us (95%)
  local copies, waits for them, and re-layouts  2.29 us (4%)
    pallas_call x1, Pallas kernels, per_device(): pl.pallas_call(functools.partial(kernel, groups, nbrs), out_shape=jax.Sha...  49.1 us
    unnamed x1, local copies, waits for them, and re-layouts  2.29 us

profile of v1, /device:TPU:0, one launch (start us, length us, event | category | flops | bytes accessed | tf_op | source)
XLA Modules:
  0.0 51.4 jit_solution(507533715690133250)
XLA Ops:
  0.0 49.1 %shard_map.37 = f32[4,256,256]{2,1,0:T(8,128)} custom-call(f32[4,256,256]{2,1,0:T(8,128)} %g_ref.1, f32[4,256,256]{2,1,0:T(8,128)} %c_ref.1, f32[256,256]{1,0:T(8,128)} %t_ref.1), custom_call_target="tpu_custom_call" | custom-call | tf_op jit(solution)/shard_map/pallas_call | solution.py:240
  49.1 2.3 %copy.5 = f32[4,256,256]{2,1,0:T(8,128)} copy(f32[4,256,256]{2,1,0:T(8,128)} %shard_map.37) | data formatting | bytes 2097152

commit v2 on v1

v2 whole, which is shorter than its diff:
```python
import functools

import jax
import jax.numpy as jnp
from jax import lax
from jax.experimental import pallas as pl
from jax.experimental.pallas import tpu as pltpu
from jax.sharding import PartitionSpec as P

MESH = pl.DeviceIdType.MESH
F32, BF16 = jnp.float32, jnp.bfloat16
PAD = 8
NN = (((1,), (0,)), ((), ()))
NT = (((1,), (1,)), ((), ()))


def halves(a):
    high = a.astype(BF16)
    return high, (a - high.astype(F32)).astype(BF16)


def left_form(a):
    high, low = halves(a)
    return jnp.concatenate([high, high, low], axis=1)


def right_form(b):
    high, low = halves(b)
    return jnp.concatenate([high, low, high], axis=0)


def right_form_tr(b):
    high, low = halves(b)
    return jnp.concatenate([high, low, high], axis=1)


def product(a, b):
    return lax.dot_general(a, b, NN, preferred_element_type=F32)


def product_tr(a, b):
    return lax.dot_general(a, b, NT, preferred_element_type=F32)


def congruence(gain, cov, state):
    mixed = product(left_form(gain), right_form(state))
    return product_tr(left_form(mixed), right_form_tr(gain)) + cov


def compose(first, second):
    gain = product(left_form(first[0]), right_form(second[0]))
    return gain, congruence(first[0], first[1], second[1])


def tree(pairs):
    while len(pairs) > 1:
        nxt = [compose(pairs[i], pairs[i + 1]) for i in range(0, len(pairs) - 1, 2)]
        if len(pairs) % 2:
            nxt.append(pairs[-1])
        pairs = nxt
    return pairs[0]


def symmetric_masks(half):
    rows = lax.broadcasted_iota(jnp.int32, (half, half), 0)
    columns = lax.broadcasted_iota(jnp.int32, (half, half), 1)
    return rows <= columns, rows == columns


def pack(ref, full):
    half = full.shape[0] // 2
    upper, diagonal = symmetric_masks(half)
    a, b, c = full[:half, :half], full[:half, half:], full[half:, half:]
    ref[0, pl.ds(0, half)] = b
    ref[1, pl.ds(0, half)] = jnp.where(upper, a, c)
    line = jnp.sum(jnp.where(diagonal, c, F32(0)), axis=0, keepdims=True)
    line = jnp.broadcast_to(line, (PAD, half))
    ref[0, pl.ds(half, PAD)] = line
    ref[1, pl.ds(half, PAD)] = line


def unpack(ref):
    half = ref.shape[2]
    upper, diagonal = symmetric_masks(half)
    b, mixed = ref[0, pl.ds(0, half)], ref[1, pl.ds(0, half)]
    line = ref[0, pl.ds(half, 1)]
    mixed_tr = mixed.T
    a = jnp.where(upper, mixed, mixed_tr)
    c = jnp.where(diagonal, line, jnp.where(upper, mixed_tr, mixed))
    return jnp.concatenate(
        [jnp.concatenate([a, b], axis=1), jnp.concatenate([b.T, c], axis=1)], axis=0
    )


def kernel(
    groups, nbrs, g_ref, c_ref, t_ref, o_ref,
    tot_e, tot_l, full_l, suf, loc, fin, state, out_state, beyond_e, beyond_l, ssem, rsem,
):
    count, width = g_ref.shape[0], g_ref.shape[1]
    half = width // 2
    quarter_len = groups // 4
    g, n = lax.axis_index("grp"), lax.axis_index("nbr")
    core = lax.rem(n, 2)
    quarter = g // quarter_len
    mate = (g, n + 1 - 2 * core)
    mine = pl.ds(pl.multiple_of(core * half, half), half)

    levels = []
    step = 1
    while step < nbrs:
        bit = lax.rem(n // step, 2)
        levels.append((bit, (g, n + step * (1 - 2 * bit))))
        step *= 2
    step = 1
    while step < quarter_len:
        bit = lax.rem(g // step, 2)
        levels.append((bit, (g + step * (1 - 2 * bit), n)))
        step *= 2
    last = len(levels)
    down = (lax.rem(g + 3 * quarter_len, groups), n)
    up = (lax.rem(g + quarter_len, groups), n)

    barrier = pltpu.get_barrier_semaphore()
    greeted = [partner for _, partner in levels] + [down, up]
    for other in greeted:
        pl.semaphore_signal(barrier, inc=1, device_id=other, device_id_type=MESH)

    sems = iter(range(ssem.shape[0]))

    def copy(src, dst, to, sem):
        return pltpu.make_async_remote_copy(
            src_ref=src, dst_ref=dst, send_sem=ssem.at[sem], recv_sem=rsem.at[sem],
            device_id=to, device_id_type=MESH,
        )

    plan = []
    for at, (bit, partner) in enumerate(levels):
        moves = []
        for ref, piece in ((tot_e, mine), (tot_l, core)):
            if at == 0:
                out = ref.at[at, bit]
                moves.append((copy(out, out, partner, next(sems)), None))
            else:
                out, came = ref.at[at, bit, piece], ref.at[at, 1 - bit, piece]
                moves.append((copy(out, out, partner, next(sems)), copy(came, came, mate, next(sems))))
        plan.append(moves)

    pending = []

    def start(move):
        move[0].start()
        pending.append(move[0])

    def arrive(move):
        move[0].wait_recv()
        if move[1] is not None:
            move[1].start()
            pending.append(move[1])
            move[1].wait_recv()

    def slot_of(at):
        return levels[at][0] if at < last else 0

    def put_cov(at, cov):
        full_l[at, slot_of(at)] = cov
        if at < last:
            pack(tot_l.at[at, slot_of(at)], cov)

    gain, cov = tree([(g_ref[k], c_ref[k]) for k in range(count)])
    tot_e[0, slot_of(0)] = gain
    put_cov(0, cov)
    pl.semaphore_wait(barrier, len(greeted))
    start(plan[0][0])
    start(plan[0][1])

    def extend_suffix(at):
        @pl.when(levels[at][0] == 0)
        def _():
            new = compose((suf[0], suf[1]), (tot_e[at, 1], full_l[at, 1]))
            suf[0], suf[1] = new

    for at, (bit, _) in enumerate(levels):
        arrive(plan[at][0])
        first = left_form(tot_e[at, 0])
        tot_e[at + 1, slot_of(at + 1)] = product(first, right_form(tot_e[at, 1]))
        if at + 1 < last:
            start(plan[at + 1][0])
        arrive(plan[at][1])
        full_l[at, 1 - bit] = unpack(tot_l.at[at, 1 - bit])
        put_cov(at + 1, congruence(tot_e[at, 0], full_l[at, 0], full_l[at, 1]))
        if at + 1 < last:
            start(plan[at + 1][1])
            if at == 0:
                own = (g_ref[count - 1], c_ref[count - 1])
                for k in range(count - 1, 0, -1):
                    if k < count - 1:
                        own = compose((g_ref[k], c_ref[k]), own)
                    loc[k, 0], loc[k, 1] = own
                loc[0, 0], loc[0, 1] = tot_e[0, slot_of(0)], full_l[0, slot_of(0)]
                rows = lax.broadcasted_iota(jnp.int32, (width, width), 0)
                columns = lax.broadcasted_iota(jnp.int32, (width, width), 1)
                suf[0] = jnp.where(rows == columns, F32(1), F32(0))
                suf[1] = jnp.zeros((width, width), F32)
            extend_suffix(at)

    total_e, total_l = tot_e.at[last, 0], full_l.at[last, 0]

    send_gain = copy(total_e.at[mine], beyond_e.at[mine], down, next(sems))
    send_cov = copy(out_state.at[core], beyond_l.at[core], down, next(sems))
    pass_gain = copy(beyond_e.at[mine], beyond_e.at[mine], mate, next(sems))
    pass_cov = copy(beyond_l.at[core], beyond_l.at[core], mate, next(sems))
    state_sem, pass_sem = next(sems), next(sems)
    send_state = copy(out_state.at[core], state.at[core], down, state_sem)
    relay_state = copy(state.at[core], state.at[core], down, state_sem)
    pass_state = copy(state.at[core], state.at[core], mate, pass_sem)

    def finals():
        for k in range(count):
            new = compose((loc[k, 0], loc[k, 1]), (suf[0], suf[1]))
            fin[k, 0], fin[k, 1] = new

    def results(entering):
        entering = right_form(entering)
        for k in range(count):
            mixed = product(left_form(fin[k, 0]), entering)
            o_ref[k] = product_tr(left_form(mixed), right_form_tr(fin[k, 0])) + fin[k, 1]

    @pl.when(quarter == 3)
    def _():
        pack(out_state, congruence(total_e[...], total_l[...], t_ref[...]))
        send_state.start()
        extend_suffix(last - 1)
        finals()
        results(t_ref[...])
        send_state.wait_send()

    @pl.when(quarter == 2)
    def _():
        extend_suffix(last - 1)
        send_state.wait_recv()
        pass_state.start()
        pass_state.wait_recv()
        pack(out_state, congruence(total_e[...], total_l[...], unpack(state)))
        send_state.start()
        finals()
        results(unpack(state))
        pass_state.wait_send()
        send_state.wait_send()

    @pl.when(quarter == 1)
    def _():
        send_gain.start()
        pack(out_state, total_l[...])
        send_cov.start()
        extend_suffix(last - 1)
        finals()
        relay_state.wait_recv()
        relay_state.start()
        pass_state.start()
        pass_state.wait_recv()
        results(unpack(state))
        pass_state.wait_send()
        send_gain.wait_send()
        send_cov.wait_send()
        relay_state.wait_send()

    @pl.when(quarter == 0)
    def _():
        extend_suffix(last - 1)
        send_gain.wait_recv()
        pass_gain.start()
        send_cov.wait_recv()
        pass_cov.start()
        pass_gain.wait()
        pass_cov.wait()
        suf[0], suf[1] = compose((suf[0], suf[1]), (beyond_e[...], unpack(beyond_l)))
        finals()
        relay_state.wait_recv()
        pass_state.start()
        pass_state.wait_recv()
        results(unpack(state))
        pass_state.wait_send()

    for one in pending:
        one.wait_send()


def solution(mesh):
    groups, nbrs = mesh.shape["grp"], mesh.shape["nbr"]
    levels = (nbrs.bit_length() - 1) + ((groups // 4).bit_length() - 1)
    n_sems = 2 + 4 * (levels - 1) + 6

    def per_device(gains, covs, terminal):
        count, width = gains.shape[0], gains.shape[1]
        pair = (2, width, width)
        packed = (2, width // 2 + PAD, width // 2)
        vmem = pl.BlockSpec(memory_space=pltpu.VMEM)
        return pl.pallas_call(
            functools.partial(kernel, groups, nbrs),
            out_shape=jax.ShapeDtypeStruct(gains.shape, F32),
            in_specs=[vmem] * 3,
            out_specs=vmem,
            scratch_shapes=[
                pltpu.VMEM((levels + 1, 2, width, width), F32),
                pltpu.VMEM((levels, 2) + packed, F32),
                pltpu.VMEM((levels + 1, 2, width, width), F32),
                pltpu.VMEM(pair, F32),
                pltpu.VMEM((count,) + pair, F32),
                pltpu.VMEM((count,) + pair, F32),
                pltpu.VMEM(packed, F32),
                pltpu.VMEM(packed, F32),
                pltpu.VMEM((width, width), F32),
                pltpu.VMEM(packed, F32),
                pltpu.SemaphoreType.DMA((n_sems,)),
                pltpu.SemaphoreType.DMA((n_sems,)),
            ],
            compiler_params=pltpu.CompilerParams(collective_id=0, has_side_effects=True),
        )(gains, covs, terminal)

    placed = P(("grp", "nbr"), None, None)
    return jax.shard_map(
        per_device, mesh=mesh, in_specs=(placed, placed, P()), out_specs=placed, check_vma=False
    )
```

time: 51.6 us -> 41.7 us (0.81)
  Pallas kernels: 49.1 us -> 38.8 us
    pallas_call x1, Pallas kernels: 49.1 us -> 38.8 us  [per_device(): pl.pallas_call(functools.partial(kernel, groups, nbrs), out_shape=jax.Sha...]
where the time goes in v2:
time: 41.7 us; the launch traced here: 41.1 us
  Pallas kernels  38.8 us (93%)
  local copies, waits for them, and re-layouts  2.29 us (5%)
    pallas_call x1, Pallas kernels, per_device(): pl.pallas_call(functools.partial(kernel, groups, nbrs), out_shape=jax.Sha...  38.8 us
    unnamed x1, local copies, waits for them, and re-layouts  2.29 us

profile of v2, /device:TPU:0, one launch (start us, length us, event | category | flops | bytes accessed | tf_op | source)
XLA Modules:
  0.0 41.1 jit_solution(18323590606324264798)
XLA Ops:
  0.0 38.8 %shard_map.37 = f32[4,256,256]{2,1,0:T(8,128)} custom-call(f32[4,256,256]{2,1,0:T(8,128)} %g_ref.1, f32[4,256,256]{2,1,0:T(8,128)} %c_ref.1, f32[256,256]{1,0:T(8,128)} %t_ref.1), custom_call_target="tpu_custom_call" | custom-call | tf_op jit(solution)/shard_map/pallas_call | solution.py:298
  38.8 2.3 %copy.5 = f32[4,256,256]{2,1,0:T(8,128)} copy(f32[4,256,256]{2,1,0:T(8,128)} %shard_map.37) | data formatting | bytes 2097152

commit v3 on v2

--- a/solution.py
+++ b/solution.py
@@ -10,6 +10,8 @@
 MESH = pl.DeviceIdType.MESH
 F32, BF16 = jnp.float32, jnp.bfloat16
 PAD = 8
+PIECES = 4
+LIMIT = 32 << 20
 NN = (((1,), (0,)), ((), ()))
 NT = (((1,), (1,)), ((), ()))
 
@@ -52,13 +54,28 @@
     return gain, congruence(first[0], first[1], second[1])
 
 
-def tree(pairs):
-    while len(pairs) > 1:
-        nxt = [compose(pairs[i], pairs[i + 1]) for i in range(0, len(pairs) - 1, 2)]
-        if len(pairs) % 2:
-            nxt.append(pairs[-1])
-        pairs = nxt
-    return pairs[0]
+def gain_tree(gains):
+    rounds = [gains]
+    while len(gains) > 1:
+        nxt = [
+            product(left_form(gains[i]), right_form(gains[i + 1])) for i in range(0, len(gains) - 1, 2)
+        ]
+        gains = nxt + gains[len(gains) - len(gains) % 2 :]
+        rounds.append(gains)
+    return rounds
+
+
+def cov_tree(rounds, covs):
+    for gains in rounds[:-1]:
+        nxt = [congruence(gains[i], covs[i], covs[i + 1]) for i in range(0, len(covs) - 1, 2)]
+        covs = nxt + covs[len(covs) - len(covs) % 2 :]
+    return covs[0]
+
+
+def pieces(rows):
+    base = rows // 8 // PIECES * 8
+    starts = [0] + [rows - base * (PIECES - i) for i in range(1, PIECES)]
+    return [(a, b - a) for a, b in zip(starts, starts[1:] + [rows])]
 
 
 def symmetric_masks(half):
@@ -93,10 +110,16 @@
 
 
 def kernel(
-    groups, nbrs, g_ref, c_ref, t_ref, o_ref,
-    tot_e, tot_l, full_l, suf, loc, fin, state, out_state, beyond_e, beyond_l, ssem, rsem,
+    groups, nbrs, g_hbm, c_hbm, t_hbm, fin, entering_ref,
+    g_ref, c_ref, t_ref, local_sem, tot_e, tot_l, full_l, suf, loc, state, out_state, beyond_e, beyond_l, ssem, rsem,
 ):
     count, width = g_ref.shape[0], g_ref.shape[1]
+    fetched = [
+        pltpu.make_async_copy(src, dst, local_sem.at[i])
+        for i, (src, dst) in enumerate(((g_hbm, g_ref), (c_hbm, c_ref), (t_hbm, t_ref)))
+    ]
+    for one in fetched:
+        one.start()
     half = width // 2
     quarter_len = groups // 4
     g, n = lax.axis_index("grp"), lax.axis_index("nbr")
@@ -166,12 +189,15 @@
         if at < last:
             pack(tot_l.at[at, slot_of(at)], cov)
 
-    gain, cov = tree([(g_ref[k], c_ref[k]) for k in range(count)])
-    tot_e[0, slot_of(0)] = gain
-    put_cov(0, cov)
+    fetched[0].wait()
+    rounds = gain_tree([g_ref[k] for k in range(count)])
+    tot_e[0, slot_of(0)] = rounds[-1][0]
     pl.semaphore_wait(barrier, len(greeted))
     start(plan[0][0])
+    fetched[1].wait()
+    put_cov(0, cov_tree(rounds, [c_ref[k] for k in range(count)]))
     start(plan[0][1])
+    fetched[2].wait()
 
     def extend_suffix(at):
         @pl.when(levels[at][0] == 0)
@@ -209,43 +235,50 @@
     send_cov = copy(out_state.at[core], beyond_l.at[core], down, next(sems))
     pass_gain = copy(beyond_e.at[mine], beyond_e.at[mine], mate, next(sems))
     pass_cov = copy(beyond_l.at[core], beyond_l.at[core], mate, next(sems))
-    state_sem, pass_sem = next(sems), next(sems)
-    send_state = copy(out_state.at[core], state.at[core], down, state_sem)
-    relay_state = copy(state.at[core], state.at[core], down, state_sem)
-    pass_state = copy(state.at[core], state.at[core], mate, pass_sem)
+    send_state, relay_state, pass_state = [], [], []
+    for begin, size in pieces(half + PAD):
+        rows = pl.ds(begin, size)
+        state_sem = next(sems)
+        send_state.append(copy(out_state.at[core, rows], state.at[core, rows], down, state_sem))
+        relay_state.append(copy(state.at[core, rows], state.at[core, rows], down, state_sem))
+        pass_state.append(copy(state.at[core, rows], state.at[core, rows], mate, next(sems)))
+
+    def receive_state(relays):
+        for i, move in enumerate(relay_state):
+            move.wait_recv()
+            if relays:
+                move.start()
+            pass_state[i].start()
+        for move in pass_state:
+            move.wait_recv()
 
     def finals():
         for k in range(count):
             new = compose((loc[k, 0], loc[k, 1]), (suf[0], suf[1]))
             fin[k, 0], fin[k, 1] = new
 
-    def results(entering):
-        entering = right_form(entering)
-        for k in range(count):
-            mixed = product(left_form(fin[k, 0]), entering)
-            o_ref[k] = product_tr(left_form(mixed), right_form_tr(fin[k, 0])) + fin[k, 1]
-
     @pl.when(quarter == 3)
     def _():
         pack(out_state, congruence(total_e[...], total_l[...], t_ref[...]))
-        send_state.start()
+        for move in send_state:
+            move.start()
+        entering_ref[...] = t_ref[...]
         extend_suffix(last - 1)
         finals()
-        results(t_ref[...])
-        send_state.wait_send()
+        for move in send_state:
+            move.wait_send()
 
     @pl.when(quarter == 2)
     def _():
         extend_suffix(last - 1)
-        send_state.wait_recv()
-        pass_state.start()
-        pass_state.wait_recv()
-        pack(out_state, congruence(total_e[...], total_l[...], unpack(state)))
-        send_state.start()
+        receive_state(False)
+        entering_ref[...] = unpack(state)
+        pack(out_state, congruence(total_e[...], total_l[...], entering_ref[...]))
+        for move in send_state:
+            move.start()
         finals()
-        results(unpack(state))
-        pass_state.wait_send()
-        send_state.wait_send()
+        for move in pass_state + send_state:
+            move.wait_send()
 
     @pl.when(quarter == 1)
     def _():
@@ -254,15 +287,10 @@
         send_cov.start()
         extend_suffix(last - 1)
         finals()
-        relay_state.wait_recv()
-        relay_state.start()
-        pass_state.start()
-        pass_state.wait_recv()
-        results(unpack(state))
-        pass_state.wait_send()
-        send_gain.wait_send()
-        send_cov.wait_send()
-        relay_state.wait_send()
+        receive_state(True)
+        entering_ref[...] = unpack(state)
+        for move in pass_state + relay_state + [send_gain, send_cov]:
+            move.wait_send()
 
     @pl.when(quarter == 0)
     def _():
@@ -275,37 +303,55 @@
         pass_cov.wait()
         suf[0], suf[1] = compose((suf[0], suf[1]), (beyond_e[...], unpack(beyond_l)))
         finals()
-        relay_state.wait_recv()
-        pass_state.start()
-        pass_state.wait_recv()
-        results(unpack(state))
-        pass_state.wait_send()
+        receive_state(False)
+        entering_ref[...] = unpack(state)
+        for move in pass_state:
+            move.wait_send()
 
     for one in pending:
         one.wait_send()
+
+
+def apply_kernel(fin, entering_ref, o_hbm, o_ref, sem):
+    count = fin.shape[0]
+    entering = right_form(entering_ref[...])
+    moves = []
+    for k in range(count):
+        mixed = product(left_form(fin[k, 0]), entering)
+        o_ref[k] = product_tr(left_form(mixed), right_form_tr(fin[k, 0])) + fin[k, 1]
+        moves.append(pltpu.make_async_copy(o_ref.at[k], o_hbm.at[k], sem.at[k]))
+        moves[-1].start()
+    for move in moves:
+        move.wait()
 
 
 def solution(mesh):
     groups, nbrs = mesh.shape["grp"], mesh.shape["nbr"]
     levels = (nbrs.bit_length() - 1) + ((groups // 4).bit_length() - 1)
-    n_sems = 2 + 4 * (levels - 1) + 6
+    n_sems = 2 + 4 * (levels - 1) + 4 + 2 * PIECES
 
     def per_device(gains, covs, terminal):
         count, width = gains.shape[0], gains.shape[1]
         pair = (2, width, width)
         packed = (2, width // 2 + PAD, width // 2)
-        vmem = pl.BlockSpec(memory_space=pltpu.VMEM)
-        return pl.pallas_call(
+        vmem, anywhere = pl.BlockSpec(memory_space=pltpu.VMEM), pl.BlockSpec(memory_space=pl.ANY)
+        maps, entering = pl.pallas_call(
             functools.partial(kernel, groups, nbrs),
-            out_shape=jax.ShapeDtypeStruct(gains.shape, F32),
-            in_specs=[vmem] * 3,
-            out_specs=vmem,
+            out_shape=(
+                jax.ShapeDtypeStruct((count,) + pair, F32),
+                jax.ShapeDtypeStruct((width, width), F32),
+            ),
+            in_specs=[pl.BlockSpec(memory_space=pltpu.HBM)] * 3,
+            out_specs=(vmem, vmem),
             scratch_shapes=[
+                pltpu.VMEM(gains.shape, F32),
+                pltpu.VMEM(gains.shape, F32),
+                pltpu.VMEM((width, width), F32),
+                pltpu.SemaphoreType.DMA((3,)),
                 pltpu.VMEM((levels + 1, 2, width, width), F32),
                 pltpu.VMEM((levels, 2) + packed, F32),
                 pltpu.VMEM((levels + 1, 2, width, width), F32),
                 pltpu.VMEM(pair, F32),
-                pltpu.VMEM((count,) + pair, F32),
                 pltpu.VMEM((count,) + pair, F32),
                 pltpu.VMEM(packed, F32),
                 pltpu.VMEM(packed, F32),
@@ -314,8 +360,18 @@
                 pltpu.SemaphoreType.DMA((n_sems,)),
                 pltpu.SemaphoreType.DMA((n_sems,)),
             ],
-            compiler_params=pltpu.CompilerParams(collective_id=0, has_side_effects=True),
-        )(gains, covs, terminal)
+            compiler_params=pltpu.CompilerParams(
+                collective_id=0, has_side_effects=True, vmem_limit_bytes=LIMIT
+            ),
+        )(*[pltpu.with_memory_space_constraint(x, pltpu.HBM) for x in (gains, covs, terminal)])
+        return pl.pallas_call(
+            apply_kernel,
+            out_shape=jax.ShapeDtypeStruct(gains.shape, F32),
+            in_specs=[vmem, vmem],
+            out_specs=anywhere,
+            scratch_shapes=[pltpu.VMEM(gains.shape, F32), pltpu.SemaphoreType.DMA((count,))],
+            compiler_params=pltpu.CompilerParams(vmem_limit_bytes=LIMIT),
+        )(maps, entering)
 
     placed = P(("grp", "nbr"), None, None)
     return jax.shard_map(

time: 41.7 us -> 37.9 us (0.909)
  local copies, waits for them, and re-layouts: 2.29 us -> 0 us
  Pallas kernels: 38.8 us -> 37.4 us
    unnamed x1 -> x0, local copies, waits for them, and re-layouts: 2.29 us -> none
    pallas_call x1 -> x2, Pallas kernels: 38.8 us -> 37.4 us  [the longest x1 35.5 us: per_device(): pl.pallas_call(functools.partial(kernel, groups, nbrs), out_shape=(jax.Sh...]
where the time goes in v3:
time: 37.9 us; the launch traced here: 37.6 us
  Pallas kernels  37.4 us (99%)
    pallas_call x1, Pallas kernels, per_device(): pl.pallas_call(functools.partial(kernel, groups, nbrs), out_shape=(jax.Sh...  35.5 us
    pallas_call x1, Pallas kernels, per_device(): pl.pallas_call(apply_kernel, out_shape=jax.ShapeDtypeStruct(gains.shape,...  1.95 us

profile of v3, /device:TPU:0, one launch (start us, length us, event | category | flops | bytes accessed | tf_op | source)
XLA Modules:
  0.0 37.6 jit_solution(16490448464460382387)
XLA Ops:
  0.0 35.5 %shard_map.37 = (f32[4,2,256,256]{3,2,1,0:T(8,128)S(1)}, f32[256,256]{1,0:T(8,128)S(1)}) custom-call(f32[4,256,256]{2,1,0:T(8,128)} %g_hbm.1, f32[4,256,256]{2,1,0:T(8,128)} %c_hbm.1, f32[256,256]{1,0:T(8,128)} %t_hbm.1), custom_call_target="tpu_custom_call" | custom-call | tf_op jit(solution)/shard_map/pallas_call | solution.py:338
  35.5 2.0 %shard_map.38 = f32[4,256,256]{2,1,0:T(8,128)} custom-call(f32[4,2,256,256]{3,2,1,0:T(8,128)S(1)} %get-tuple-element.7.fin, f32[256,256]{1,0:T(8,128)S(1)} %get-tuple-element.8.entering_ref), custom_call_target="tpu_custom_call" | custom-call | tf_op jit(solution)/shard_map/pallas_call | solution.py:367

commit v4 on v3

--- a/solution.py
+++ b/solution.py
@@ -111,7 +111,7 @@
 
 def kernel(
     groups, nbrs, g_hbm, c_hbm, t_hbm, fin, entering_ref,
-    g_ref, c_ref, t_ref, local_sem, tot_e, tot_l, full_l, suf, loc, state, out_state, beyond_e, beyond_l, ssem, rsem,
+    g_ref, c_ref, t_ref, local_sem, tot_e, tot_l, full_l, quad_e, quad_l, quad_full, two_e, two_l, suf, loc, state, out_state, beyond_e, beyond_l, ssem, rsem,
 ):
     count, width = g_ref.shape[0], g_ref.shape[1]
     fetched = [
@@ -128,23 +128,33 @@
     mate = (g, n + 1 - 2 * core)
     mine = pl.ds(pl.multiple_of(core * half, half), half)
 
-    levels = []
+    bits = []
     step = 1
     while step < nbrs:
         bit = lax.rem(n // step, 2)
-        levels.append((bit, (g, n + step * (1 - 2 * bit))))
+        bits.append((bit, (0, step * (1 - 2 * bit))))
         step *= 2
+    joint = len(bits) - 1
     step = 1
     while step < quarter_len:
         bit = lax.rem(g // step, 2)
-        levels.append((bit, (g + step * (1 - 2 * bit), n)))
+        bits.append((bit, (step * (1 - 2 * bit), 0)))
         step *= 2
+    partners = [(g + a, n + b) for _, (a, b) in bits]
+    levels = [(bits[i][0], partners[i]) for i in range(joint)]
+    levels.append(None)
+    levels += [(bits[i][0], partners[i]) for i in range(joint + 2, len(bits))]
     last = len(levels)
+    low, high = bits[joint][0], bits[joint + 1][0]
+    own_slot = 2 * high + low
+    low_slot, high_slot, far_slot = 2 * high + 1 - low, 2 * (1 - high) + low, 2 * (1 - high) + 1 - low
+    relay_slot = low_slot + core * (high_slot - low_slot)
+    relay_to = (g + (1 - core) * bits[joint + 1][1][0], n + core * bits[joint][1][1])
     down = (lax.rem(g + 3 * quarter_len, groups), n)
     up = (lax.rem(g + quarter_len, groups), n)
 
     barrier = pltpu.get_barrier_semaphore()
-    greeted = [partner for _, partner in levels] + [down, up]
+    greeted = partners + [down, up]
     for other in greeted:
         pl.semaphore_signal(barrier, inc=1, device_id=other, device_id_type=MESH)
 
@@ -157,9 +167,20 @@
         )
 
     plan = []
-    for at, (bit, partner) in enumerate(levels):
+    for at, level in enumerate(levels):
         moves = []
-        for ref, piece in ((tot_e, mine), (tot_l, core)):
+        for ref, quad, piece in ((tot_e, quad_e, mine), (tot_l, quad_l, core)):
+            if level is None:
+                out = quad.at[own_slot, piece]
+                move = [copy(out, out, partners[joint + i], next(sems)) for i in range(2)]
+                out = quad.at[relay_slot, piece]
+                move.append(copy(out, out, relay_to, next(sems)))
+                for slot in (low_slot, high_slot, far_slot):
+                    out = quad.at[slot, piece]
+                    move.append(copy(out, out, mate, next(sems)))
+                moves.append(move)
+                continue
+            bit, partner = level
             if at == 0:
                 out = ref.at[at, bit]
                 moves.append((copy(out, out, partner, next(sems)), None))
@@ -170,63 +191,121 @@
 
     pending = []
 
-    def start(move):
-        move[0].start()
-        pending.append(move[0])
+    def start(at, what):
+        if at < last:
+            for one in plan[at][what][: 2 if levels[at] is None else 1]:
+                one.start()
+                pending.append(one)
+
+    def go(one):
+        one.start()
+        pending.append(one)
 
     def arrive(move):
         move[0].wait_recv()
         if move[1] is not None:
-            move[1].start()
-            pending.append(move[1])
+            go(move[1])
             move[1].wait_recv()
 
-    def slot_of(at):
-        return levels[at][0] if at < last else 0
+    def arrive_near(move):
+        move[0].wait_recv()
+        move[1].wait_recv()
+        for one in move[2:5]:
+            go(one)
+        for one in move[3:5]:
+            one.wait_recv()
+
+    def arrive_far(move):
+        move[2].wait_recv()
+        go(move[5])
+        move[5].wait_recv()
+
+    def put_gain(at, gain):
+        if at < last and levels[at] is None:
+            quad_e[own_slot] = gain
+        else:
+            tot_e[at, levels[at][0] if at < last else 0] = gain
 
     def put_cov(at, cov):
-        full_l[at, slot_of(at)] = cov
-        if at < last:
-            pack(tot_l.at[at, slot_of(at)], cov)
+        if at < last and levels[at] is None:
+            quad_full[own_slot] = cov
+            pack(quad_l.at[own_slot], cov)
+        elif at < last:
+            full_l[at, levels[at][0]] = cov
+            pack(tot_l.at[at, levels[at][0]], cov)
+        else:
+            full_l[at, 0] = cov
 
     fetched[0].wait()
     rounds = gain_tree([g_ref[k] for k in range(count)])
-    tot_e[0, slot_of(0)] = rounds[-1][0]
+    put_gain(0, rounds[-1][0])
+    loc[0, 0] = rounds[-1][0]
     pl.semaphore_wait(barrier, len(greeted))
-    start(plan[0][0])
+    start(0, 0)
     fetched[1].wait()
-    put_cov(0, cov_tree(rounds, [c_ref[k] for k in range(count)]))
-    start(plan[0][1])
+    cov = cov_tree(rounds, [c_ref[k] for k in range(count)])
+    put_cov(0, cov)
+    loc[0, 1] = cov
+    start(0, 1)
     fetched[2].wait()
 
+    def local_suffixes():
+        own = (g_ref[count - 1], c_ref[count - 1])
+        for k in range(count - 1, 0, -1):
+            if k < count - 1:
+                own = compose((g_ref[k], c_ref[k]), own)
+            loc[k, 0], loc[k, 1] = own
+        rows = lax.broadcasted_iota(jnp.int32, (width, width), 0)
+        columns = lax.broadcasted_iota(jnp.int32, (width, width), 1)
+        suf[0] = jnp.where(rows == columns, F32(1), F32(0))
+        suf[1] = jnp.zeros((width, width), F32)
+
+    def lengthen(bit, gain_ref, cov_ref):
+        @pl.when(bit == 0)
+        def _():
+            suf[0], suf[1] = compose((suf[0], suf[1]), (gain_ref[...], cov_ref[...]))
+
     def extend_suffix(at):
-        @pl.when(levels[at][0] == 0)
-        def _():
-            new = compose((suf[0], suf[1]), (tot_e[at, 1], full_l[at, 1]))
-            suf[0], suf[1] = new
-
-    for at, (bit, _) in enumerate(levels):
-        arrive(plan[at][0])
-        first = left_form(tot_e[at, 0])
-        tot_e[at + 1, slot_of(at + 1)] = product(first, right_form(tot_e[at, 1]))
+        if levels[at] is None:
+            lengthen(low, quad_e.at[2 * high + 1], quad_full.at[2 * high + 1])
+            lengthen(high, two_e.at[1], two_l.at[1])
+        else:
+            lengthen(levels[at][0], tot_e.at[at, 1], full_l.at[at, 1])
+
+    def pair_gain(which):
+        two_e[which] = product(left_form(quad_e[2 * which]), right_form(quad_e[2 * which + 1]))
+
+    def pair_cov(which):
+        two_l[which] = congruence(quad_e[2 * which], quad_full[2 * which], quad_full[2 * which + 1])
+
+    for at, level in enumerate(levels):
+        if level is None:
+            gain_moves, cov_moves = plan[at]
+            arrive_near(gain_moves)
+            pair_gain(high)
+            arrive_near(cov_moves)
+            for slot in (low_slot, high_slot):
+                quad_full[slot] = unpack(quad_l.at[slot])
+            pair_cov(high)
+            arrive_far(gain_moves)
+            pair_gain(1 - high)
+            put_gain(at + 1, product(left_form(two_e[0]), right_form(two_e[1])))
+            start(at + 1, 0)
+            arrive_far(cov_moves)
+            quad_full[far_slot] = unpack(quad_l.at[far_slot])
+            pair_cov(1 - high)
+            put_cov(at + 1, congruence(two_e[0], two_l[0], two_l[1]))
+        else:
+            arrive(plan[at][0])
+            put_gain(at + 1, product(left_form(tot_e[at, 0]), right_form(tot_e[at, 1])))
+            start(at + 1, 0)
+            arrive(plan[at][1])
+            full_l[at, 1 - level[0]] = unpack(tot_l.at[at, 1 - level[0]])
+            put_cov(at + 1, congruence(tot_e[at, 0], full_l[at, 0], full_l[at, 1]))
+        start(at + 1, 1)
         if at + 1 < last:
-            start(plan[at + 1][0])
-        arrive(plan[at][1])
-        full_l[at, 1 - bit] = unpack(tot_l.at[at, 1 - bit])
-        put_cov(at + 1, congruence(tot_e[at, 0], full_l[at, 0], full_l[at, 1]))
-        if at + 1 < last:
-            start(plan[at + 1][1])
             if at == 0:
-                own = (g_ref[count - 1], c_ref[count - 1])
-                for k in range(count - 1, 0, -1):
-                    if k < count - 1:
-                        own = compose((g_ref[k], c_ref[k]), own)
-                    loc[k, 0], loc[k, 1] = own
-                loc[0, 0], loc[0, 1] = tot_e[0, slot_of(0)], full_l[0, slot_of(0)]
-                rows = lax.broadcasted_iota(jnp.int32, (width, width), 0)
-                columns = lax.broadcasted_iota(jnp.int32, (width, width), 1)
-                suf[0] = jnp.where(rows == columns, F32(1), F32(0))
-                suf[1] = jnp.zeros((width, width), F32)
+                local_suffixes()
             extend_suffix(at)
 
     total_e, total_l = tot_e.at[last, 0], full_l.at[last, 0]
@@ -327,8 +406,8 @@
 
 def solution(mesh):
     groups, nbrs = mesh.shape["grp"], mesh.shape["nbr"]
-    levels = (nbrs.bit_length() - 1) + ((groups // 4).bit_length() - 1)
-    n_sems = 2 + 4 * (levels - 1) + 4 + 2 * PIECES
+    levels = (nbrs.bit_length() - 1) + ((groups // 4).bit_length() - 1) - 1
+    n_sems = 2 + 4 * (levels - 2) + 12 + 4 + 2 * PIECES
 
     def per_device(gains, covs, terminal):
         count, width = gains.shape[0], gains.shape[1]
@@ -351,6 +430,11 @@
                 pltpu.VMEM((levels + 1, 2, width, width), F32),
                 pltpu.VMEM((levels, 2) + packed, F32),
                 pltpu.VMEM((levels + 1, 2, width, width), F32),
+                pltpu.VMEM((4, width, width), F32),
+                pltpu.VMEM((4,) + packed, F32),
+                pltpu.VMEM((4, width, width), F32),
+                pltpu.VMEM(pair, F32),
+                pltpu.VMEM(pair, F32),
                 pltpu.VMEM(pair, F32),
                 pltpu.VMEM((count,) + pair, F32),
                 pltpu.VMEM(packed, F32),

time: 37.9 us -> 36.4 us (0.960)
  Pallas kernels: 37.4 us -> 36 us
    pallas_call x1, Pallas kernels: 35.5 us -> 34.1 us  [per_device(): pl.pallas_call(functools.partial(kernel, groups, nbrs), out_shape=(jax.Sh...]
where the time goes in v4:
time: 36.4 us; the launch traced here: 36.2 us
  Pallas kernels  36 us (99%)
    pallas_call x1, Pallas kernels, per_device(): pl.pallas_call(functools.partial(kernel, groups, nbrs), out_shape=(jax.Sh...  34.1 us
    pallas_call x1, Pallas kernels, per_device(): pl.pallas_call(apply_kernel, out_shape=jax.ShapeDtypeStruct(gains.shape,...  1.95 us

profile of v4, /device:TPU:0, one launch (start us, length us, event | category | flops | bytes accessed | tf_op | source)
XLA Modules:
  0.0 36.2 jit_solution(12617972839211930262)
XLA Ops:
  0.0 34.1 %shard_map.37 = (f32[4,2,256,256]{3,2,1,0:T(8,128)S(1)}, f32[256,256]{1,0:T(8,128)S(1)}) custom-call(f32[4,256,256]{2,1,0:T(8,128)} %g_hbm.1, f32[4,256,256]{2,1,0:T(8,128)} %c_hbm.1, f32[256,256]{1,0:T(8,128)} %t_hbm.1), custom_call_target="tpu_custom_call" | custom-call | tf_op jit(solution)/shard_map/pallas_call | solution.py:417
  34.1 2.0 %shard_map.38 = f32[4,256,256]{2,1,0:T(8,128)} custom-call(f32[4,2,256,256]{3,2,1,0:T(8,128)S(1)} %get-tuple-element.7.fin, f32[256,256]{1,0:T(8,128)S(1)} %get-tuple-element.8.entering_ref), custom_call_target="tpu_custom_call" | custom-call | tf_op jit(solution)/shard_map/pallas_call | solution.py:451

commit v5 on v4

--- a/solution.py
+++ b/solution.py
@@ -272,6 +272,12 @@
         else:
             lengthen(levels[at][0], tot_e.at[at, 1], full_l.at[at, 1])
 
+    def apply_early(at):
+        if at + 1 == last:
+            gain = tot_e[last, 0]
+            mixed = product(left_form(gain), right_form(t_ref[...]))
+            entering_ref[...] = product_tr(left_form(mixed), right_form_tr(gain))
+
     def pair_gain(which):
         two_e[which] = product(left_form(quad_e[2 * which]), right_form(quad_e[2 * which + 1]))
 
@@ -291,6 +297,7 @@
             pair_gain(1 - high)
             put_gain(at + 1, product(left_form(two_e[0]), right_form(two_e[1])))
             start(at + 1, 0)
+            apply_early(at)
             arrive_far(cov_moves)
             quad_full[far_slot] = unpack(quad_l.at[far_slot])
             pair_cov(1 - high)
@@ -299,14 +306,11 @@
             arrive(plan[at][0])
             put_gain(at + 1, product(left_form(tot_e[at, 0]), right_form(tot_e[at, 1])))
             start(at + 1, 0)
+            apply_early(at)
             arrive(plan[at][1])
             full_l[at, 1 - level[0]] = unpack(tot_l.at[at, 1 - level[0]])
             put_cov(at + 1, congruence(tot_e[at, 0], full_l[at, 0], full_l[at, 1]))
         start(at + 1, 1)
-        if at + 1 < last:
-            if at == 0:
-                local_suffixes()
-            extend_suffix(at)
 
     total_e, total_l = tot_e.at[last, 0], full_l.at[last, 0]
 
@@ -338,18 +342,29 @@
 
     @pl.when(quarter == 3)
     def _():
-        pack(out_state, congruence(total_e[...], total_l[...], t_ref[...]))
+        pack(out_state, entering_ref[...] + total_l[...])
         for move in send_state:
             move.start()
+
+    @pl.when(quarter == 1)
+    def _():
+        send_gain.start()
+        pack(out_state, total_l[...])
+        send_cov.start()
+
+    local_suffixes()
+    for at in range(last):
+        extend_suffix(at)
+
+    @pl.when(quarter == 3)
+    def _():
         entering_ref[...] = t_ref[...]
-        extend_suffix(last - 1)
         finals()
         for move in send_state:
             move.wait_send()
 
     @pl.when(quarter == 2)
     def _():
-        extend_suffix(last - 1)
         receive_state(False)
         entering_ref[...] = unpack(state)
         pack(out_state, congruence(total_e[...], total_l[...], entering_ref[...]))
@@ -361,10 +376,6 @@
 
     @pl.when(quarter == 1)
     def _():
-        send_gain.start()
-        pack(out_state, total_l[...])
-        send_cov.start()
-        extend_suffix(last - 1)
         finals()
         receive_state(True)
         entering_ref[...] = unpack(state)
@@ -373,7 +384,6 @@
 
     @pl.when(quarter == 0)
     def _():
-        extend_suffix(last - 1)
         send_gain.wait_recv()
         pass_gain.start()
         send_cov.wait_recv()

time: 36.4 us -> 36.4 us (level)
  no operation moved by 1% of the time
where the time goes in v5:
time: 36.4 us; the launch traced here: 36.2 us
  Pallas kernels  36.1 us (99%)
    pallas_call x1, Pallas kernels, per_device(): pl.pallas_call(functools.partial(kernel, groups, nbrs), out_shape=(jax.Sh...  34.1 us
    pallas_call x1, Pallas kernels, per_device(): pl.pallas_call(apply_kernel, out_shape=jax.ShapeDtypeStruct(gains.shape,...  1.95 us

profile of v5, /device:TPU:0, one launch (start us, length us, event | category | flops | bytes accessed | tf_op | source)
XLA Modules:
  0.0 36.2 jit_solution(5665594735894984463)
XLA Ops:
  0.0 34.1 %shard_map.37 = (f32[4,2,256,256]{3,2,1,0:T(8,128)S(1)}, f32[256,256]{1,0:T(8,128)S(1)}) custom-call(f32[4,256,256]{2,1,0:T(8,128)} %g_hbm.1, f32[4,256,256]{2,1,0:T(8,128)} %c_hbm.1, f32[256,256]{1,0:T(8,128)} %t_hbm.1), custom_call_target="tpu_custom_call" | custom-call | tf_op jit(solution)/shard_map/pallas_call | solution.py:427
  34.1 1.9 %shard_map.38 = f32[4,256,256]{2,1,0:T(8,128)} custom-call(f32[4,2,256,256]{3,2,1,0:T(8,128)S(1)} %get-tuple-element.7.fin, f32[256,256]{1,0:T(8,128)S(1)} %get-tuple-element.8.entering_ref), custom_call_target="tpu_custom_call" | custom-call | tf_op jit(solution)/shard_map/pallas_call | solution.py:461
